TPU v7x, 32 devices: a whole 2x2x4 slice. The times are simulated.
32 devices in a mesh: parts: 2 (over y), patch: 4 (over z), level: 2 (over x), sub: 2 (over core).
Axes of the slice: x: 2, y: 2, z: 4, core: 2. Of those that a mesh axis runs over, the one named last changes fastest.
Arguments:
- adjoint_height: float32 [4, 1024, 1024], P(('parts', 'level'), ('patch', 'sub')), parts along dimension 0, may hold values from -6 to 6
- adjoint_momenta: float32 [2, 4, 1024, 1024], P(None, ('parts', 'level'), ('patch', 'sub')), parts along dimension 1, may hold values from -6 to 6
- depth: float32 [2, 1024, 1024], P('level', ('patch', 'sub')), may hold values from 0.2 to 1
- wet_mask: int32 [2, 1024, 1024], P('level', ('patch', 'sub')), may hold values 0 or 1
- adjacency: int32 [2, 4, 4], P('level'), may hold values from -1 to 3, as said below
- nest_gain: float32 [2, 8192], P(None, ('patch', 'sub')), may hold values from 0.75 to 1
- nest_index: int32 [2, 8192], P(None, ('patch', 'sub')), may hold values from 0 to 1023, as said below
Outputs:
- height_out: float32 [4, 1024, 1024], P(('parts', 'level'), ('patch', 'sub')), parts along dimension 0
- momenta_out: float32 [2, 4, 1024, 1024], P(None, ('parts', 'level'), ('patch', 'sub')), parts along dimension 1
There are 2 independent parts, one for each index of `parts`. A program takes and returns all parts, laid end to end along the dimension named above; an argument that names none is the same for every part. Nothing has to cross between parts.
Inputs may be any that keep to these rules, and one draw needn't show every extreme that they name: `adjacency`: the patches of a level sit on a grid of cells in an order drawn from the seed; each row of a patch lists its grid neighbours, -1 at the grid's edge, and neighbour links are symmetric. `nest_index`: entries index a cell of the same half patch's strip, 1024 cells long.
All inputs are finite; a program needn't handle non-finite values. No bound on the sum of `wet_mask` on one device may be relied on, other than what follows from the above.
Results may differ from a plain program's by a relative error of at most 0.00002.
Values sent between devices are 32-bit elements; how exact they have to be, the bound alone decides.
A program may use at most 64 MiB of HBM per device.

v0:
```python
import jax
import jax.numpy as jnp
from jax import lax
from jax.sharding import PartitionSpec as P

STEPS = 2
courant = 0.45


def passed_along(value, axis, steps):
    count = lax.axis_size(axis)
    initial, last = (max(0, -steps), min(count, count - steps))
    return lax.ppermute(value, axis, [(source, source + steps) for source in range(initial, last)])


def pick_row(table, index):
    return lax.dynamic_index_in_dim(table, index, 0, keepdims=False)


def body(adjoint_height, adjoint_momenta, depth, wet_mask, adjacency, nest_gain, nest_index):
    eta = adjoint_height[0]
    mom_row = adjoint_momenta[0, 0]
    mom_col = adjoint_momenta[1, 0]
    height = depth[0]
    wet = wet_mask[0].astype(jnp.float32)
    level = lax.axis_index("level")
    patch = lax.axis_index("patch")
    half = lax.axis_index("sub")
    levels = lax.axis_size("level")
    subs = lax.axis_size("sub")
    segments = lax.axis_size("patch") * subs
    links = pick_row(adjacency[0], patch)
    north = links[0]
    south = links[1]
    west = links[2]
    east = links[3]
    has_north = (north >= 0).astype(jnp.float32)
    has_south = (south >= 0).astype(jnp.float32)
    has_west = (west >= 0).astype(jnp.float32)
    has_east = (east >= 0).astype(jnp.float32)
    own_gain = pick_row(nest_gain, level)
    own_table = pick_row(nest_index, level)
    for step in range(STEPS):
        strip = eta[0]
        flux = strip
        inflow = jnp.zeros_like(strip)
        for turn in range(levels - 1):
            received = passed_along(flux, "level", -1)
            inflow = own_gain * jnp.take(received, own_table)
            flux = inflow + strip
        eta = eta.at[0].add(inflow)
        first_col = eta[:, 0]
        first_row = eta[0, :]
        east_cols = lax.all_gather(first_col[None], ("patch", "sub"), axis=0, tiled=True)
        east_rows = lax.all_gather(first_row[None], ("patch", "sub"), axis=0, tiled=True)
        east_col = jnp.take(east_cols, jnp.maximum(east, 0) * subs + half, axis=0) * has_east
        east_inside = jnp.take(
            east_rows, jnp.minimum(patch * subs + half + 1, segments - 1), axis=0
        )
        east_across = jnp.take(east_rows, jnp.maximum(south, 0) * subs, axis=0) * has_south
        south_row = jnp.where(half == subs - 1, east_across, east_inside)
        east_col, south_row = (east_col, south_row)
        east_eta = jnp.concatenate([eta[:, 1:], east_col[:, None]], axis=1)
        south_eta = jnp.concatenate([eta[1:], south_row[None]], axis=0)
        mom_row = wet * (mom_row - courant * (east_eta - eta))
        mom_col = wet * (mom_col - courant * (south_eta - eta))
        last_col = mom_row[:, -1]
        last_row = mom_col[-1, :]
        cols = lax.all_gather(last_col[None], ("patch", "sub"), axis=0, tiled=True)
        rows = lax.all_gather(last_row[None], ("patch", "sub"), axis=0, tiled=True)
        west_col = jnp.take(cols, jnp.maximum(west, 0) * subs + half, axis=0) * has_west
        inside = jnp.take(rows, jnp.maximum(patch * subs + half - 1, 0), axis=0)
        across = jnp.take(rows, jnp.maximum(north, 0) * subs + subs - 1, axis=0) * has_north
        north_row = jnp.where(half == 0, across, inside)
        west_col, north_row = (west_col, north_row)
        west_row = jnp.concatenate([west_col[:, None], mom_row[:, :-1]], axis=1)
        north_col = jnp.concatenate([north_row[None], mom_col[:-1]], axis=0)
        eta = wet * (eta - courant * height * (mom_row - west_row + (mom_col - north_col)))
    return (eta[None], jnp.stack([mom_row, mom_col])[:, None])


def solution(mesh):
    in_specs = (
        P(("parts", "level"), ("patch", "sub"), None),
        P(None, ("parts", "level"), ("patch", "sub"), None),
        P("level", ("patch", "sub"), None),
        P("level", ("patch", "sub"), None),
        P("level", None, None),
        P(None, ("patch", "sub")),
        P(None, ("patch", "sub")),
    )
    out_specs = (
        P(("parts", "level"), ("patch", "sub"), None),
        P(None, ("parts", "level"), ("patch", "sub"), None),
    )
    return jax.shard_map(body, mesh=mesh, in_specs=in_specs, out_specs=out_specs, check_vma=False)
```

profile of v0, /device:TPU:0, one launch (start us, length us, event | category | flops | bytes accessed | tf_op | source)
XLA Modules:
  0.0 152.6 jit_solution(2689515999720986161)
XLA Ops:
  0.6 0.0 copy-start
  0.6 1.0 copy.33
  1.7 1.3 collective-permute-start
  3.0 0.7 constant_dynamic-slice_fusion.4
  3.7 0.6 fusion.35
  4.3 0.0 copy-done
  4.3 0.0 copy-start.4
  4.3 0.7 copy-done.4
  10.1 0.0 collective-permute-done
  10.2 4.5 %gather_fusion = f32[1024]{0:T(1024)S(1)} fusion(f32[1024]{0:T(1024)S(1)} %collective-permute-done, s32[1024]{0:T(1024)S(1)} %fusion.22), kind=kCustom, calls=%fused_computation.clone | custom fusion | bytes 12288 | tf_op jit(solution)/shard_map/jit(_take)/gather | solution.py:49
  14.7 15.7 %all-gather.2 = f32[8192]{0:T(1024)S(1)} all-gather(f32[1024]{0:T(1024)S(1)} %get-tuple-element.51), channel_id=4, replica_groups=mesh['parts'=2,'patch'=4,'level'=2,'sub'=2] {'patch','sub'}, dimensions={0}, use_global_device_ids=true | all-gather | bytes 36864 | tf_op jit(solution)/shard_map/all_gather | solution.py:55
  30.4 0.1 scatter-add.6
  30.5 0.2 slice.143
  30.7 0.0 copy-start.1
  30.8 14.8 %all-gather = f32[1024,1]{1,0:T(8,128)S(1)} all-gather(f32[128,1]{1,0:T(8,128)S(1)} %slice.144), channel_id=2, replica_groups=mesh['parts'=2,'patch'=4,'level'=2,'sub'=2] {'patch','sub'}, dimensions={0}, use_global_device_ids=true | all-gather | bytes 4608 | tf_op jit(solution)/shard_map/all_gather | solution.py:54
  45.6 0.2 reduce.4
  45.8 0.1 copy.17
  46.0 0.0 copy-done.1
  46.0 1.6 %fusion.9 = (f32[128,1024]{1,0:T(8,128)S(1)}, f32[128,1024]{1,0:T(8,128)S(1)}) fusion(f32[128,1024]{1,0:T(8,128)S(1)} %scatter-add.6, f32[1,1024]{1,0:T(1,128)S(1)} %bitcast.119, f32[127,1024]{1,0:T(8,128)S(1)} %slice.147, f32[2,1,128,1024]{3,2,1,0:T(8,128)} %param.18, s32[1,128,1024]{2,1,0:T(8,128)S(1)} %copy-done.1, f32[128,1]{1,0:T(8,128)S(1)} %copy.17, ...), kind=kLoop, calls=%fused_computation.15 | loop fusion | flops 1441792 | bytes 4194304 | tf_op jit(solution)/shard_map/mul | solution.py:66
  47.6 14.2 %all-gather.5 = f32[8,1,1024]{2,1,0:T(1,128)S(1)} all-gather(f32[1,1,1024]{2,1,0:T(1,128)S(1)} %slice_bitcast_fusion.1), channel_id=1, replica_groups=mesh['parts'=2,'patch'=4,'level'=2,'sub'=2] {'patch','sub'}, dimensions={0}, use_global_device_ids=true | all-gather | bytes 36864 | tf_op jit(solution)/shard_map/all_gather | solution.py:70
  61.8 0.1 slice.145
  61.9 0.0 copy-start.2
  61.9 15.0 %all-gather.1 = f32[1024,1]{1,0:T(8,128)S(1)} all-gather(f32[128,1]{1,0:T(8,128)S(1)} %slice.145), channel_id=3, replica_groups=mesh['parts'=2,'patch'=4,'level'=2,'sub'=2] {'patch','sub'}, dimensions={0}, use_global_device_ids=true | all-gather | bytes 4608 | tf_op jit(solution)/shard_map/all_gather | solution.py:69
  76.9 0.2 reduce.5
  77.2 0.1 copy.18
  77.3 0.0 copy-done.2
  77.3 0.4 fusion.6
  77.7 1.3 collective-permute-start.1
  79.0 4.2 %collective-permute-done.1 = f32[1024]{0:T(1024)S(1)} collective-permute-done((f32[1024]{0:T(1024)S(1)}, f32[1024]{0:T(1024)S(1)}, u32[]{:S(2)}, u32[]{:S(2)}) %collective-permute-start.1) | collective-permute-done | bytes 4128 | tf_op jit(solution)/shard_map/ppermute | solution.py:13
  83.2 4.5 %gather_fusion.1 = f32[1024]{0:T(1024)S(1)} fusion(f32[1024]{0:T(1024)S(1)} %collective-permute-done.1, s32[1024]{0:T(1024)S(1)} %fusion.22), kind=kCustom, calls=%fused_computation.1.clone | custom fusion | bytes 12288 | tf_op jit(solution)/shard_map/jit(_take)/gather | solution.py:49
  87.8 0.1 scatter-add.9
  87.9 0.8 slice.155
  88.8 1.0 slice.151
  89.8 14.0 %all-gather.6 = f32[8,1,1024]{2,1,0:T(1,128)S(1)} all-gather(f32[1,1,1024]{2,1,0:T(1,128)S(1)} %bitcast.111), channel_id=1, replica_groups=mesh['parts'=2,'patch'=4,'level'=2,'sub'=2] {'patch','sub'}, dimensions={0}, use_global_device_ids=true | all-gather | bytes 36864 | tf_op jit(solution)/shard_map/all_gather | solution.py:55
  103.8 14.9 %all-gather.3 = f32[1024,1]{1,0:T(8,128)S(1)} all-gather(f32[128,1]{1,0:T(8,128)S(1)} %slice.152), channel_id=5, replica_groups=mesh['parts'=2,'patch'=4,'level'=2,'sub'=2] {'patch','sub'}, dimensions={0}, use_global_device_ids=true | all-gather | bytes 4608 | tf_op jit(solution)/shard_map/all_gather | solution.py:54
  118.7 0.2 reduce.6
  118.9 0.1 copy.19
  119.1 1.6 %fusion.20 = (f32[128,1024]{1,0:T(8,128)S(1)}, f32[128,1024]{1,0:T(8,128)S(1)}) fusion(f32[128,1024]{1,0:T(8,128)S(1)} %get-tuple-element.53, f32[128,1024]{1,0:T(8,128)S(1)} %scatter-add.9, f32[1,1024]{1,0:T(1,128)S(1)} %bitcast.117, f32[127,1024]{1,0:T(8,128)} %slice.155, s32[1,128,1024]{2,1,0:T(8,128)S(1)} %copy-done.1, ...), kind=kLoop, calls=%fused_computation.30 | loop fusion | flops 1441792 | bytes 4194304 | tf_op jit(solution)/shard_map/mul | solution.py:66
  120.6 14.3 %all-gather.7 = f32[8,1,1024]{2,1,0:T(1,128)S(1)} all-gather(f32[1,1,1024]{2,1,0:T(1,128)S(1)} %slice_bitcast_fusion), channel_id=1, replica_groups=mesh['parts'=2,'patch'=4,'level'=2,'sub'=2] {'patch','sub'}, dimensions={0}, use_global_device_ids=true | all-gather | bytes 36864 | tf_op jit(solution)/shard_map/all_gather | solution.py:70
  134.9 0.1 slice.153
  135.0 14.9 %all-gather.4 = f32[1024,1]{1,0:T(8,128)S(1)} all-gather(f32[128,1]{1,0:T(8,128)S(1)} %slice.153), channel_id=6, replica_groups=mesh['parts'=2,'patch'=4,'level'=2,'sub'=2] {'patch','sub'}, dimensions={0}, use_global_device_ids=true | all-gather | bytes 4608 | tf_op jit(solution)/shard_map/all_gather | solution.py:69
  149.9 0.2 reduce.7
  150.1 0.1 copy.20
  150.2 0.0 copy-start.3
  150.3 1.1 maximum_bitcast_fusion
  151.3 0.1 copy-done.3
  151.4 1.2 fusion.17
  (29 shorter events, 0.3 us)
Async XLA Ops:
  0.6 3.7 %copy-start = (s32[2,1024]{1,0:T(2,128)S(1)}, s32[2,1024]{1,0:T(2,128)}, u32[]{:S(2)}) copy-start(s32[2,1024]{1,0:T(2,128)} %param.23) | copy-start | bytes 24580
  1.7 8.4 %collective-permute-start = (f32[1024]{0:T(1024)S(1)}, f32[1024]{0:T(1024)S(1)}, u32[]{:S(2)}, u32[]{:S(2)}) collective-permute-start(f32[1024]{0:T(1024)S(1)} %bitcast.122), channel_id=1, source_target_pairs={{2,0},{3,1},{6,4},{7,5},{10,8},{11,9},{14,12},{15,13},{18,16},{19,... | collective-permute-start | bytes 12296 | tf_op jit(solution)/shard_map/ppermute | solution.py:13
  4.3 0.7 copy-start.4
  30.7 15.2 %copy-start.1 = (s32[1,128,1024]{2,1,0:T(8,128)S(1)}, s32[1,128,1024]{2,1,0:T(8,128)}, u32[]{:S(2)}) copy-start(s32[1,128,1024]{2,1,0:T(8,128)} %param.20) | copy-start | bytes 1572868
  61.9 15.4 %copy-start.2 = (f32[1,128,1024]{2,1,0:T(8,128)S(1)}, f32[1,128,1024]{2,1,0:T(8,128)}, u32[]{:S(2)}) copy-start(f32[1,128,1024]{2,1,0:T(8,128)} %param.19) | copy-start | bytes 1572868
  77.7 5.5 %collective-permute-start.1 = (f32[1024]{0:T(1024)S(1)}, f32[1024]{0:T(1024)S(1)}, u32[]{:S(2)}, u32[]{:S(2)}) collective-permute-start(f32[1024]{0:T(1024)S(1)} %bitcast.136), channel_id=1, source_target_pairs={{2,0},{3,1},{6,4},{7,5},{10,8},{11,9},{14,12},{15,13},{18,16},{19,... | collective-permute-start | bytes 12296 | tf_op jit(solution)/shard_map/ppermute | solution.py:13
  150.2 1.1 copy-start.3
where the time goes:
time: 153 us
  blocking collectives  118 us (77%)
  local copies, waits for them, and re-layouts  15.1 us (10%)
  other arithmetic  6.77 us (4%)
  between operations  6.05 us (4%)
  waiting for transfers between devices  4.2 us (3%)
  starting transfers between devices  2.57 us (2%)
    all_gather x2, blocking collectives, body(): cols = lax.all_gather(last_col[None], ('patch', 'sub'), axis=0, tiled=True)  29.9 us
    all_gather x2, blocking collectives, body(): lax.all_gather(first_col[None], ('patch', 'sub'), axis=0, tiled=True)  29.8 us
    all_gather x2, blocking collectives, body(): lax.all_gather(first_row[None], ('patch', 'sub'), axis=0, tiled=True)  29.7 us
    all_gather x2, blocking collectives, body(): rows = lax.all_gather(last_row[None], ('patch', 'sub'), axis=0, tiled=True)  28.5 us
    gather x2, local copies, waits for them, and re-layouts, body(): inflow = own_gain * jnp.take(received, own_table)  9.05 us
    ppermute x2, waiting for transfers between devices, passed_along(): lax.ppermute(value, axis, [(source, source + steps) for source in range(i...  4.2 us
    mul x2, other arithmetic, body(): mom_col = wet * (mom_col - courant * (south_eta - eta))  3.13 us
  transfers between devices with their start and end apart: 2, of which 1 were waited for; matrix products, arithmetic and copies ran while one was open for 1% of the time, Pallas kernels for 0%

commit v1 on v0

--- a/solution.py
+++ b/solution.py
@@ -5,6 +5,25 @@
 
 STEPS = 2
 courant = 0.45
+
+
+def in_order(blocks, dim):
+    shape = list(blocks.shape[1:])
+    shape[dim] *= blocks.shape[0]
+    return jnp.moveaxis(blocks, 0, dim).reshape(shape)
+
+
+def grow_blocks(x, axis):
+    length, index = (lax.axis_size(axis), lax.axis_index(axis))
+    blocks, bit = (x[None], 1)
+    while bit < length:
+        received = lax.ppermute(blocks, axis, [(i, i ^ bit) for i in range(length)])
+        low = index & bit == 0
+        blocks = jnp.concatenate(
+            [jnp.where(low, blocks, received), jnp.where(low, received, blocks)]
+        )
+        bit *= 2
+    return blocks
 
 
 def passed_along(value, axis, steps):
@@ -67,7 +86,7 @@
         last_col = mom_row[:, -1]
         last_row = mom_col[-1, :]
         cols = lax.all_gather(last_col[None], ("patch", "sub"), axis=0, tiled=True)
-        rows = lax.all_gather(last_row[None], ("patch", "sub"), axis=0, tiled=True)
+        rows = in_order(grow_blocks(last_row[None], ("patch", "sub")), 0)
         west_col = jnp.take(cols, jnp.maximum(west, 0) * subs + half, axis=0) * has_west
         inside = jnp.take(rows, jnp.maximum(patch * subs + half - 1, 0), axis=0)
         across = jnp.take(rows, jnp.maximum(north, 0) * subs + subs - 1, axis=0) * has_north

time: 153 us -> 138 us (0.902)
  blocking collectives: 118 us -> 88.9 us
  waiting for transfers between devices: 4.2 us -> 13.6 us
  starting transfers between devices: 2.57 us -> 6.78 us
    all_gather x2 -> x0, blocking collectives: 28.5 us -> none  [body(): rows = lax.all_gather(last_row[None], ('patch', 'sub'), axis=0, tiled=True)]
    ppermute x0 -> x6, waiting for transfers between devices: none -> 9.38 us  [grow_blocks(): received = lax.ppermute(blocks, axis, [(i, i ^ bit) for i in range(length)])]
    ppermute x0 -> x6, starting transfers between devices: none -> 4.21 us  [grow_blocks(): received = lax.ppermute(blocks, axis, [(i, i ^ bit) for i in range(length)])]
  transfers between devices with their start and end apart: 2 -> 8, of which waited for: 1 -> 5; matrix products, arithmetic and copies ran while one was open for 1% -> 2% of each run, Pallas kernels for 0% -> 0%
where the time goes in v1:
time: 138 us
  blocking collectives  88.9 us (64%)
  local copies, waits for them, and re-layouts  15.1 us (11%)
  waiting for transfers between devices  13.6 us (10%)
  other arithmetic  6.91 us (5%)
  starting transfers between devices  6.78 us (5%)
  between operations  6.21 us (4%)
    all_gather x2, blocking collectives, body(): lax.all_gather(first_row[None], ('patch', 'sub'), axis=0, tiled=True)  29.7 us
    all_gather x2, blocking collectives, body(): lax.all_gather(first_col[None], ('patch', 'sub'), axis=0, tiled=True)  29.7 us
    all_gather x2, blocking collectives, body(): cols = lax.all_gather(last_col[None], ('patch', 'sub'), axis=0, tiled=True)  29.6 us
    ppermute x6, waiting for transfers between devices, grow_blocks(): received = lax.ppermute(blocks, axis, [(i, i ^ bit) for i in range(length)])  9.38 us
    gather x2, local copies, waits for them, and re-layouts, body(): inflow = own_gain * jnp.take(received, own_table)  9.05 us
    ppermute x6, starting transfers between devices, grow_blocks(): received = lax.ppermute(blocks, axis, [(i, i ^ bit) for i in range(length)])  4.21 us
    ppermute x2, waiting for transfers between devices, passed_along(): lax.ppermute(value, axis, [(source, source + steps) for source in range(i...  4.2 us
    mul x2, other arithmetic, body(): mom_col = wet * (mom_col - courant * (south_eta - eta))  3.13 us
  transfers between devices with their start and end apart: 8, of which 5 were waited for; matrix products, arithmetic and copies ran while one was open for 2% of the time, Pallas kernels for 0%

profile of v1, /device:TPU:0, one launch (start us, length us, event | category | flops | bytes accessed | tf_op | source)
XLA Modules:
  0.0 137.5 jit_solution(8471939332566619102)
XLA Ops:
  0.6 0.0 copy-start
  0.6 1.0 copy.27
  1.7 1.3 collective-permute-start
  3.0 0.7 constant_dynamic-slice_fusion.4
  3.7 0.7 fusion.35
  4.3 0.0 copy-done
  4.3 0.0 copy-start.4
  4.4 0.7 copy-done.4
  7.7 0.0 collective-permute-done
  7.7 4.5 %gather_fusion = f32[1024]{0:T(1024)S(1)} fusion(f32[1024]{0:T(1024)S(1)} %collective-permute-done, s32[1024]{0:T(1024)S(1)} %fusion.22), kind=kCustom, calls=%fused_computation.clone | custom fusion | bytes 12288 | tf_op jit(solution)/shard_map/jit(_take)/gather | solution.py:68
  12.2 15.7 %all-gather.2 = f32[8192]{0:T(1024)S(1)} all-gather(f32[1024]{0:T(1024)S(1)} %get-tuple-element.51), channel_id=4, replica_groups=mesh['parts'=2,'patch'=4,'level'=2,'sub'=2] {'patch','sub'}, dimensions={0}, use_global_device_ids=true | all-gather | bytes 36864 | tf_op jit(solution)/shard_map/all_gather | solution.py:74
  27.9 0.1 scatter-add.6
  28.0 0.2 slice.143
  28.3 0.0 copy-start.1
  28.3 14.8 %all-gather = f32[1024,1]{1,0:T(8,128)S(1)} all-gather(f32[128,1]{1,0:T(8,128)S(1)} %slice.144), channel_id=2, replica_groups=mesh['parts'=2,'patch'=4,'level'=2,'sub'=2] {'patch','sub'}, dimensions={0}, use_global_device_ids=true | all-gather | bytes 4608 | tf_op jit(solution)/shard_map/all_gather | solution.py:73
  43.1 0.2 reduce.4
  43.3 0.1 copy.17
  43.5 0.0 copy-done.1
  43.5 1.6 %fusion.9 = (f32[128,1024]{1,0:T(8,128)S(1)}, f32[128,1024]{1,0:T(8,128)S(1)}) fusion(f32[128,1024]{1,0:T(8,128)S(1)} %scatter-add.6, f32[1,1024]{1,0:T(1,128)S(1)} %bitcast.123, f32[127,1024]{1,0:T(8,128)S(1)} %slice.147, f32[2,1,128,1024]{3,2,1,0:T(8,128)} %param.18, s32[1,128,1024]{2,1,0:T(8,128)S(1)} %copy-done.1, f32[128,1]{1,0:T(8,128)S(1)} %copy.17, ...), kind=kLoop, calls=%fused_computation.15 | loop fusion | flops 1441792 | bytes 4194304 | tf_op jit(solution)/shard_map/mul | solution.py:85
  45.1 0.4 collective-permute-start.1
  45.5 0.8 collective-permute-done.1
  46.4 1.9 %collective-permute-start.2 = (f32[2,1,1024]{2,0,1:T(2,128)S(1)}, f32[2,1,1024]{2,0,1:T(2,128)S(1)}, u32[]{:S(2)}, u32[]{:S(2)}) collective-permute-start(f32[2,1,1024]{2,0,1:T(2,128)S(1)} %pad_maximum_fusion.2), channel_id=1, source_target_pairs={{0,4},{1,5},{4,0},{5,1},{8,12},{9,13},{12,8},{13,9},{2,6},{3,7},{6... | collective-permute-start | bytes 24584 | tf_op jit(solution)/shard_map/ppermute | solution.py:20
  50.8 0.1 slice.145
  50.9 14.8 %all-gather.1 = f32[1024,1]{1,0:T(8,128)S(1)} all-gather(f32[128,1]{1,0:T(8,128)S(1)} %slice.145), channel_id=3, replica_groups=mesh['parts'=2,'patch'=4,'level'=2,'sub'=2] {'patch','sub'}, dimensions={0}, use_global_device_ids=true | all-gather | bytes 4608 | tf_op jit(solution)/shard_map/all_gather | solution.py:88
  65.7 0.0 copy-start.2
  65.7 0.2 reduce.5
  65.9 0.0 collective-permute-done.2
  66.0 0.7 collective-permute-start.3
  66.7 0.1 copy.18
  66.8 3.9 %collective-permute-done.3 = f32[4,1,1024]{2,0,1:T(4,128)S(1)} collective-permute-done((f32[4,1,1024]{2,0,1:T(4,128)S(1)}, f32[4,1,1024]{2,0,1:T(4,128)S(1)}, u32[]{:S(2)}, u32[]{:S(2)}) %collective-permute-start.3) | collective-permute-done | bytes 16416 | tf_op jit(solution)/shard_map/ppermute | solution.py:20
  70.7 0.0 copy-done.2
  70.7 0.4 fusion.6
  71.2 1.3 collective-permute-start.4
  72.5 4.2 %collective-permute-done.4 = f32[1024]{0:T(1024)S(1)} collective-permute-done((f32[1024]{0:T(1024)S(1)}, f32[1024]{0:T(1024)S(1)}, u32[]{:S(2)}, u32[]{:S(2)}) %collective-permute-start.4) | collective-permute-done | bytes 4128 | tf_op jit(solution)/shard_map/ppermute | solution.py:32
  76.7 4.5 %gather_fusion.1 = f32[1024]{0:T(1024)S(1)} fusion(f32[1024]{0:T(1024)S(1)} %collective-permute-done.4, s32[1024]{0:T(1024)S(1)} %fusion.22), kind=kCustom, calls=%fused_computation.1.clone | custom fusion | bytes 12288 | tf_op jit(solution)/shard_map/jit(_take)/gather | solution.py:68
  81.2 0.1 scatter-add.9
  81.4 0.8 slice.155
  82.2 1.0 slice.151
  83.2 14.0 %all-gather.5 = f32[8,1,1024]{2,1,0:T(1,128)S(1)} all-gather(f32[1,1,1024]{2,1,0:T(1,128)S(1)} %bitcast.115), channel_id=1, replica_groups=mesh['parts'=2,'patch'=4,'level'=2,'sub'=2] {'patch','sub'}, dimensions={0}, use_global_device_ids=true | all-gather | bytes 36864 | tf_op jit(solution)/shard_map/all_gather | solution.py:74
  97.2 14.8 %all-gather.3 = f32[1024,1]{1,0:T(8,128)S(1)} all-gather(f32[128,1]{1,0:T(8,128)S(1)} %slice.152), channel_id=5, replica_groups=mesh['parts'=2,'patch'=4,'level'=2,'sub'=2] {'patch','sub'}, dimensions={0}, use_global_device_ids=true | all-gather | bytes 4608 | tf_op jit(solution)/shard_map/all_gather | solution.py:73
  112.0 0.2 reduce.6
  112.3 0.1 copy.19
  112.4 1.6 %fusion.20 = (f32[128,1024]{1,0:T(8,128)S(1)}, f32[128,1024]{1,0:T(8,128)S(1)}) fusion(f32[128,1024]{1,0:T(8,128)S(1)} %get-tuple-element.53, f32[128,1024]{1,0:T(8,128)S(1)} %scatter-add.9, f32[1,1024]{1,0:T(1,128)S(1)} %bitcast.121, f32[127,1024]{1,0:T(8,128)} %slice.155, s32[1,128,1024]{2,1,0:T(8,128)S(1)} %copy-done.1, ...), kind=kLoop, calls=%fused_computation.30 | loop fusion | flops 1441792 | bytes 4194304 | tf_op jit(solution)/shard_map/mul | solution.py:85
  114.0 0.4 collective-permute-start.5
  114.4 0.8 collective-permute-done.5
  115.2 0.1 collective-permute-start.6
  115.3 1.0 maximum_bitcast_fusion
  116.3 0.1 slice.153
  116.4 14.8 %all-gather.4 = f32[1024,1]{1,0:T(8,128)S(1)} all-gather(f32[128,1]{1,0:T(8,128)S(1)} %slice.153), channel_id=6, replica_groups=mesh['parts'=2,'patch'=4,'level'=2,'sub'=2] {'patch','sub'}, dimensions={0}, use_global_device_ids=true | all-gather | bytes 4608 | tf_op jit(solution)/shard_map/all_gather | solution.py:88
  131.2 0.0 copy-start.3
  131.2 0.2 reduce.7
  131.4 0.0 collective-permute-done.6
  131.5 0.7 collective-permute-start.7
  132.2 0.1 copy.20
  132.3 3.9 %collective-permute-done.7 = f32[4,1,1024]{2,0,1:T(4,128)S(1)} collective-permute-done((f32[4,1,1024]{2,0,1:T(4,128)S(1)}, f32[4,1,1024]{2,0,1:T(4,128)S(1)}, u32[]{:S(2)}, u32[]{:S(2)}) %collective-permute-start.7) | collective-permute-done | bytes 16416 | tf_op jit(solution)/shard_map/ppermute | solution.py:20
  136.3 0.0 copy-done.3
  136.3 1.2 fusion.17
  (39 shorter events, 0.4 us)
Async XLA Ops:
  0.6 3.7 %copy-start = (s32[2,1024]{1,0:T(2,128)S(1)}, s32[2,1024]{1,0:T(2,128)}, u32[]{:S(2)}) copy-start(s32[2,1024]{1,0:T(2,128)} %param.23) | copy-start | bytes 24580
  1.7 6.0 %collective-permute-start = (f32[1024]{0:T(1024)S(1)}, f32[1024]{0:T(1024)S(1)}, u32[]{:S(2)}, u32[]{:S(2)}) collective-permute-start(f32[1024]{0:T(1024)S(1)} %bitcast.126), channel_id=1, source_target_pairs={{2,0},{3,1},{6,4},{7,5},{10,8},{11,9},{14,12},{15,13},{18,16},{19,... | collective-permute-start | bytes 12296 | tf_op jit(solution)/shard_map/ppermute | solution.py:32
  4.3 0.7 copy-start.4
  28.3 15.2 %copy-start.1 = (s32[1,128,1024]{2,1,0:T(8,128)S(1)}, s32[1,128,1024]{2,1,0:T(8,128)}, u32[]{:S(2)}) copy-start(s32[1,128,1024]{2,1,0:T(8,128)} %param.20) | copy-start | bytes 1572868
  45.1 1.2 collective-permute-start.1
  46.4 19.5 %collective-permute-start.2 = (f32[2,1,1024]{2,0,1:T(2,128)S(1)}, f32[2,1,1024]{2,0,1:T(2,128)S(1)}, u32[]{:S(2)}, u32[]{:S(2)}) collective-permute-start(f32[2,1,1024]{2,0,1:T(2,128)S(1)} %pad_maximum_fusion.2), channel_id=1, source_target_pairs={{0,4},{1,5},{4,0},{5,1},{8,12},{9,13},{12,8},{13,9},{2,6},{3,7},{6... | collective-permute-start | bytes 24584 | tf_op jit(solution)/shard_map/ppermute | solution.py:20
  65.7 5.0 %copy-start.2 = (f32[1,128,1024]{2,1,0:T(8,128)S(1)}, f32[1,128,1024]{2,1,0:T(8,128)}, u32[]{:S(2)}) copy-start(f32[1,128,1024]{2,1,0:T(8,128)} %param.19) | copy-start | bytes 1572868
  66.0 4.7 %collective-permute-start.3 = (f32[4,1,1024]{2,0,1:T(4,128)S(1)}, f32[4,1,1024]{2,0,1:T(4,128)S(1)}, u32[]{:S(2)}, u32[]{:S(2)}) collective-permute-start(f32[4,1,1024]{2,0,1:T(4,128)S(1)} %pad_maximum_fusion), channel_id=1, source_target_pairs={{0,8},{1,9},{4,12},{5,13},{8,0},{9,1},{12,4},{13,5},{2,10},{3,11},... | collective-permute-start | bytes 49160 | tf_op jit(solution)/shard_map/ppermute | solution.py:20
  71.2 5.5 %collective-permute-start.4 = (f32[1024]{0:T(1024)S(1)}, f32[1024]{0:T(1024)S(1)}, u32[]{:S(2)}, u32[]{:S(2)}) collective-permute-start(f32[1024]{0:T(1024)S(1)} %bitcast.140), channel_id=1, source_target_pairs={{2,0},{3,1},{6,4},{7,5},{10,8},{11,9},{14,12},{15,13},{18,16},{19,... | collective-permute-start | bytes 12296 | tf_op jit(solution)/shard_map/ppermute | solution.py:32
  114.0 1.2 collective-permute-start.5
  115.2 16.2 %collective-permute-start.6 = (f32[2,1,1024]{2,0,1:T(2,128)S(1)}, f32[2,1,1024]{2,0,1:T(2,128)S(1)}, u32[]{:S(2)}, u32[]{:S(2)}) collective-permute-start(f32[2,1,1024]{2,0,1:T(2,128)S(1)} %pad_maximum_fusion.3), channel_id=1, source_target_pairs={{0,4},{1,5},{4,0},{5,1},{8,12},{9,13},{12,8},{13,9},{2,6},{3,7},{6... | collective-permute-start | bytes 24584 | tf_op jit(solution)/shard_map/ppermute | solution.py:20
  131.2 5.0 %copy-start.3 = (f32[1,128,1024]{2,1,0:T(8,128)S(1)}, f32[1,128,1024]{2,1,0:T(8,128)}, u32[]{:S(2)}) copy-start(f32[1,128,1024]{2,1,0:T(8,128)} %param.19) | copy-start | bytes 1572868
  131.5 4.7 %collective-permute-start.7 = (f32[4,1,1024]{2,0,1:T(4,128)S(1)}, f32[4,1,1024]{2,0,1:T(4,128)S(1)}, u32[]{:S(2)}, u32[]{:S(2)}) collective-permute-start(f32[4,1,1024]{2,0,1:T(4,128)S(1)} %pad_maximum_fusion.1), channel_id=1, source_target_pairs={{0,8},{1,9},{4,12},{5,13},{8,0},{9,1},{12,4},{13,5},{2,10},{3,11},... | collective-permute-start | bytes 49160 | tf_op jit(solution)/shard_map/ppermute | solution.py:20
